TPU v7x, 128 devices: a whole 4x4x4 slice. The times are simulated.
128 devices in a mesh: fsdp: 16 (over x, z), dp: 8 (over y, core).
Axes of the slice: x: 4, y: 4, z: 4, core: 2. Of those that a mesh axis runs over, the one named last changes fastest.
Arguments:
- grad_parts: bfloat16 [8, 16384, 2048], P('dp', 'fsdp'), may hold values from -6 to 6
- old_master: float32 [16384, 2048], P(('fsdp', 'dp')), may hold values from -0.25 to 0.25
- old_mean: bfloat16 [16384, 2048], P(('fsdp', 'dp')), may hold values from -1 to 1
- old_mean_scale: bfloat16 [16384], P(('fsdp', 'dp')), may hold values from 0.049804688 to 0.5
- old_square: bfloat16 [16384, 2048], P(('fsdp', 'dp')), may hold values from 0.049804688 to 1
- old_square_scale: bfloat16 [16384], P(('fsdp', 'dp')), may hold values from 0.29882812 to 3
- old_map: int32 [16384], replicated, may hold values from 0 to 16383, as said below
Outputs:
- weights: bfloat16 [16384, 2048], P('fsdp')
- master: float32 [16384, 2048], P(('fsdp', 'dp'))
- mean_codes: bfloat16 [16384, 2048], P(('fsdp', 'dp'))
- mean_scales: bfloat16 [16384], P(('fsdp', 'dp'))
- square_codes: bfloat16 [16384, 2048], P(('fsdp', 'dp'))
- square_scales: bfloat16 [16384], P(('fsdp', 'dp'))
Inputs may be any that keep to these rules, and one draw needn't show every extreme that they name: old_map is a permutation of the old slots; old slot s lies on device s // 128 counted along fsdp+dp with fsdp major, and block b belongs to new owner b // 128 counted the same way. Every device holds exactly 128 old slots; one device holds at most 2 blocks of one new owner, and every draw has a pair with exactly 2.
All inputs are finite; a program needn't handle non-finite values. Where the computation divides by a largest or mean magnitude, that divisor is 1e-20 or more.
Results may differ from a plain program's by a relative error of at most 0.02.
Values may be sent and summed in bfloat16 or wider, within the bound.
No kernel may reach another device: no remote copies, remote signals or barrier semaphores. Data moves between devices by JAX's collectives and lax.ppermute only.
A program may use at most 64 MiB of HBM per device.

v0:
```python
import jax
import jax.numpy as jnp
from jax import lax
from jax.sharding import PartitionSpec as P


def pair_rank(owners, keyed):
    matching = owners[:, None] == owners[None, :]
    before = keyed[None, :] < keyed[:, None]
    return jnp.sum(jnp.where(matching & before, 1, 0), axis=1).astype(jnp.int32)


def route_bf16(chooser, values):
    flat_values = values.reshape((values.shape[0], -1))
    moved = jnp.dot(chooser.astype(jnp.bfloat16), flat_values, preferred_element_type=jnp.float32)
    return moved.astype(jnp.bfloat16).reshape((chooser.shape[0],) + values.shape[1:])


def route_f32(chooser, values):
    return jnp.dot(
        chooser.astype(jnp.float32),
        values,
        precision=lax.Precision.HIGHEST,
        preferred_element_type=jnp.float32,
    )


def block_peak(values):
    return (jnp.max(values, axis=1) + 1e-06).astype(jnp.bfloat16)


def local(grad_parts, old_master, old_mean, old_mean_scale, old_square, old_square_scale, old_map):
    count_all = lax.axis_size(("fsdp", "dp"))
    block_rows = old_master.shape[0]
    block_len = old_master.shape[1]
    peer_cap = max(2, 2 * block_rows // count_all)
    slot_total = count_all * peer_cap
    self_index = lax.axis_index(("fsdp", "dp"))
    gradient = lax.psum_scatter(
        grad_parts[0].astype(jnp.float32).astype(jnp.bfloat16),
        "dp",
        scatter_dimension=0,
        tiled=True,
    ).astype(jnp.float32)
    total_blocks = old_map.shape[0]
    my_slots = self_index * block_rows + jnp.arange(block_rows, dtype=jnp.int32)
    block_ids = jnp.arange(total_blocks, dtype=jnp.int32)
    held_blocks = jnp.sum(
        jnp.where(old_map[None, :] == my_slots[:, None], block_ids[None, :], 0), axis=1
    )
    target = held_blocks // block_rows
    local_pos = held_blocks % block_rows
    sent_rank = pair_rank(target, local_pos)
    wanted = lax.dynamic_slice_in_dim(old_map, self_index * block_rows, block_rows)
    source = wanted // block_rows
    got_rank = pair_rank(source, jnp.arange(block_rows, dtype=jnp.int32))
    slot_ids = jnp.arange(slot_total, dtype=jnp.int32)
    send_flat = target * peer_cap + sent_rank
    placing = slot_ids[:, None] == send_flat[None, :]
    moment_codes = jnp.stack([old_mean, old_square], axis=1)
    moment_scales = jnp.stack([old_mean_scale, old_square_scale], axis=1)
    code_buffer = route_bf16(placing, moment_codes).reshape((count_all, peer_cap, 2, block_len))
    scale_buffer = route_bf16(placing, moment_scales).reshape((count_all, peer_cap, 2))
    master_buffer = route_f32(placing, old_master).reshape((count_all, peer_cap, block_len))
    code_in, scale_in = (
        lax.all_to_all(code_buffer, ("fsdp", "dp"), split_axis=0, concat_axis=0, tiled=True),
        lax.all_to_all(scale_buffer, ("fsdp", "dp"), split_axis=0, concat_axis=0, tiled=True),
    )
    master_in = lax.all_to_all(
        master_buffer.astype(jnp.bfloat16), ("fsdp", "dp"), split_axis=0, concat_axis=0, tiled=True
    ).astype(master_buffer.dtype)
    recv_flat = source * peer_cap + got_rank
    picking = recv_flat[:, None] == slot_ids[None, :]
    code_rows = route_bf16(picking, code_in.reshape((slot_total, 2, block_len))).astype(jnp.float32)
    scale_rows = route_bf16(picking, scale_in.reshape((slot_total, 2))).astype(jnp.float32)
    weight_old = route_f32(picking, master_in.reshape((slot_total, block_len)))
    mean_old = code_rows[:, 0] * scale_rows[:, 0:1]
    square_old = code_rows[:, 1] * scale_rows[:, 1:2]
    mean_next = 0.9 * mean_old + 0.1 * gradient
    square_next = 0.95 * square_old + 0.05 * gradient * gradient
    master = weight_old - 0.05 * (mean_next / (jnp.sqrt(square_next) + 1e-08) + 0.1 * weight_old)
    mean_scales = block_peak(jnp.abs(mean_next))
    square_scales = block_peak(square_next)
    mean_codes = (mean_next / mean_scales.astype(jnp.float32)[:, None]).astype(jnp.bfloat16)
    square_codes = (square_next / square_scales.astype(jnp.float32)[:, None]).astype(jnp.bfloat16)
    weights = lax.all_gather(master.astype(jnp.bfloat16), "dp", axis=0, tiled=True)
    return (weights, master, mean_codes, mean_scales, square_codes, square_scales)


def solution(mesh):
    in_specs = (
        P("dp", "fsdp", None),
        P(("fsdp", "dp"), None),
        P(("fsdp", "dp"), None),
        P(("fsdp", "dp")),
        P(("fsdp", "dp"), None),
        P(("fsdp", "dp")),
        P(),
    )
    out_specs = (
        P("fsdp", None),
        P(("fsdp", "dp"), None),
        P(("fsdp", "dp"), None),
        P(("fsdp", "dp")),
        P(("fsdp", "dp"), None),
        P(("fsdp", "dp")),
    )
    return jax.shard_map(local, mesh=mesh, in_specs=in_specs, out_specs=out_specs, check_vma=False)
```

profile of v0, /device:TPU:1, one launch (start us, length us, event | category | flops | bytes accessed | tf_op | source)
XLA Modules:
  0.0 145.3 jit_solution(600305273660461602)
XLA Ops:
  7.2 0.0 copy-start
  7.2 0.0 reduce-scatter.2.cloned.1.call-start
  7.2 0.0 copy-start.4
  7.2 0.0 copy-start.5
  7.2 0.0 copy-start.6
  7.3 0.7 reduce-scatter.2.cloned.1.call-update
  7.9 0.2 copy-done.4
  8.1 1.3 select_reduce_fusion
  9.5 0.2 select_reduce_fusion.1
  9.7 0.1 convolution_convert_fusion.3
  9.8 0.2 reshape.115
  10.0 0.7 copy.29
  10.7 11.5 %all-to-all-start.2 = ((bf16[128,2,2]{1,2,0:T(2,128)(2,1)}), bf16[128,2,2]{1,2,0:T(2,128)(2,1)S(1)}, u32[]{:S(2)}, u32[]{:S(2)}) async-start(bf16[128,2,2]{1,2,0:T(2,128)(2,1)} %copy.29), calls=%async_computation.2 | async-start | bytes 131072 | tf_op jit(solution)/shard_map/all_to_all | solution.py:67
  22.2 1.0 convolution_convert_fusion.2
  23.3 0.0 copy-start.2
  23.3 0.0 copy-start.3
  23.3 1.5 %convert_element_type.77 = bf16[128,2,2048]{2,1,0:T(2,128)(2,1)} reshape(bf16[256,2048]{1,0:T(8,128)(2,1)S(1)} %convolution_convert_fusion.2) | data formatting | bytes 2097152 | tf_op jit(solution)/shard_map/convert_element_type | solution.py:70
  24.8 6.9 %all-to-all-done.2 = bf16[128,2,2]{1,2,0:T(2,128)(2,1)S(1)} async-done(((bf16[128,2,2]{1,2,0:T(2,128)(2,1)}), bf16[128,2,2]{1,2,0:T(2,128)(2,1)S(1)}, u32[]{:S(2)}, u32[]{:S(2)}) %all-to-all-start.2) | async-done | bytes 1056 | tf_op jit(solution)/shard_map/all_to_all | solution.py:67
  31.7 5.4 %all-to-all-start = ((bf16[128,2,2048]{2,1,0:T(2,128)(2,1)}), bf16[128,2,2048]{2,1,0:T(2,128)(2,1)}, u32[]{:S(2)}, u32[]{:S(2)}) async-start(bf16[128,2,2048]{2,1,0:T(2,128)(2,1)} %convert_element_type.77), calls=%async_computation | async-start | bytes 2097152 | tf_op jit(solution)/shard_map/all_to_all | solution.py:69
  37.0 0.3 copy.25
  37.3 0.3 copy.26
  37.6 0.1 pad_maximum_fusion
  37.7 0.7 convolution_convert_fusion
  38.4 2.8 %reshape_reshape.6 = bf16[128,2,2,2048]{3,2,1,0:T(2,128)(2,1)} reshape(bf16[256,4096]{1,0:T(8,128)(2,1)S(1)} %convolution_convert_fusion) | data formatting | bytes 4194304 | tf_op jit(solution)/shard_map/reshape;reshape | solution.py:62
  41.2 14.7 %all-to-all-done = bf16[128,2,2048]{2,1,0:T(2,128)(2,1)} async-done(((bf16[128,2,2048]{2,1,0:T(2,128)(2,1)}), bf16[128,2,2048]{2,1,0:T(2,128)(2,1)}, u32[]{:S(2)}, u32[]{:S(2)}) %all-to-all-start) | async-done | bytes 1048608 | tf_op jit(solution)/shard_map/all_to_all | solution.py:69
  55.9 5.8 %all-to-all-start.1 = ((bf16[128,2,2,2048]{3,2,1,0:T(2,128)(2,1)}), bf16[128,2,2,2048]{3,2,1,0:T(2,128)(2,1)S(1)}, u32[]{:S(2)}, u32[]{:S(2)}) async-start(bf16[128,2,2,2048]{3,2,1,0:T(2,128)(2,1)} %reshape_reshape.6), calls=%async_computation.1 | async-start | bytes 4194304 | tf_op jit(solution)/shard_map/all_to_all | solution.py:66
  61.7 0.2 all-gather.2.cloned.1.call-start
  61.9 0.1 and_select_fusion.2
  62.0 0.2 select_reduce_fusion.2
  62.2 0.1 multiply_add_fusion.1
  62.3 0.1 reshape.116
  62.4 0.2 fusion.1
  62.6 2.3 %reshape.113 = bf16[256,2048]{1,0:T(8,128)(2,1)} reshape(bf16[128,2,2048]{2,1,0:T(2,128)(2,1)} %all-to-all-done) | data formatting | bytes 2097152 | tf_op jit(solution)/shard_map/reshape | solution.py:76
  64.9 27.1 %all-to-all-done.1 = bf16[128,2,2,2048]{3,2,1,0:T(2,128)(2,1)S(1)} async-done(((bf16[128,2,2,2048]{3,2,1,0:T(2,128)(2,1)}), bf16[128,2,2,2048]{3,2,1,0:T(2,128)(2,1)S(1)}, u32[]{:S(2)}, u32[]{:S(2)}) %all-to-all-start.1) | async-done | bytes 2097184 | tf_op jit(solution)/shard_map/all_to_all | solution.py:66
  92.1 0.9 copy.34
  93.0 1.8 %fusion = f32[128,4096]{1,0:T(8,128)} fusion(bf16[256,4096]{1,0:T(8,128)(2,1)S(1)} %bitcast.49, s32[128]{0:T(128)S(1)} %multiply_add_fusion.1), kind=kOutput, calls=%fused_computation.3 | convolution fusion | flops 269516800 | bytes 4194816 | tf_op jit(solution)/shard_map/dot_general | solution.py:15
  94.8 1.9 %copy.27 = f32[128,4096]{0,1:T(8,128)S(1)} copy(f32[128,4096]{1,0:T(8,128)} %fusion) | data formatting | bytes 4194304 | tf_op jit(solution)/shard_map/convert_element_type | solution.py:74
  96.7 1.5 fusion.21
  98.1 1.6 %copy.33 = f32[128,1,2048]{2,0,1:T(8,128)S(1)} copy(f32[128,1,2048]{0,2,1:T(8,128)} %get-tuple-element.12) | data formatting | bytes 2097152
  99.7 1.6 %copy.32 = f32[128,1,2048]{2,0,1:T(8,128)S(1)} copy(f32[128,1,2048]{0,2,1:T(8,128)} %get-tuple-element.13) | data formatting | bytes 2097152
  101.3 0.0 reduce-scatter.2.cloned.1.call-done
  101.3 3.5 %fusion.22 = (bf16[128,2048]{1,0:T(8,128)(2,1)}, f32[128,2048]{1,0:T(8,128)}) fusion(f32[128]{0:T(128)S(1)} %get-tuple-element.16, f32[128,1,2048]{2,0,1:T(8,128)S(1)} %copy.33, bf16[128,2048]{1,0:T(8,128)(2,1)} %reduce-scatter.2.cloned.1.call-done, f32[128]{0:T(128)S(1)} %get-tuple-element.17, f32[128,1,2048]{2,0,1:T(8,128)S(1)} %copy.32, ...), kind=kOutput, calls=%fused_computation.58 | convolution fusion | flops 138706944 | bytes 5244416 | tf_op jit(solution)/shard_map/dot_general | solution.py:20
  104.8 0.0 all-gather.2.cloned.1.call-update
  104.9 1.7 %fusion.18 = (f32[128]{0:T(128)S(1)}, f32[128]{0:T(128)S(1)}) fusion(bf16[128,2048]{1,0:T(8,128)(2,1)} %reduce-scatter.2.cloned.1.call-done, f32[128]{0:T(128)S(1)} %get-tuple-element.16, f32[128,1,2048]{2,0,1:T(8,128)S(1)} %copy.33, f32[128]{0:T(128)S(1)} %get-tuple-element.17, f32[128,1,2048]{2,0,1:T(8,128)S(1)} %copy.32), kind=kLoop, calls=%fused_computation.54 | loop fusion | flops 3407616 | bytes 2623488 | tf_op jit(solution)/shard_map/reduce_max | solution.py:29
  106.5 0.5 fusion.19
  107.1 1.4 divide_convert_fusion
  108.5 25.1 %all-gather.2.cloned.1.call-done = bf16[1024,2048]{1,0:T(8,128)(2,1)} async-done(((bf16[128,2048]{1,0:T(8,128)(2,1)}), bf16[1024,2048]{1,0:T(8,128)(2,1)}) %all-gather.2.cloned.1.call-update) | async-done | bytes 4194320 | tf_op jit(solution)/shard_map/all_gather | solution.py:86
  133.6 4.8 %copy.36 = bf16[1024,2048]{1,0:T(8,128)(2,1)} copy(bf16[1024,2048]{1,0:T(8,128)(2,1)} %all-gather.2.cloned.1.call-done) | data formatting | bytes 8388608
  (12 shorter events, 0.1 us)
Async XLA Ops:
  7.2 15.1 %copy-start = (f32[128,2048]{1,0:T(8,128)S(1)}, f32[128,2048]{1,0:T(8,128)}, u32[]{:S(2)}) copy-start(f32[128,2048]{1,0:T(8,128)} %param.8) | copy-start | bytes 3145732
  7.2 94.1 %reduce-scatter.2.cloned.1.call-start = ((), (), s32[]{:S(2)}) async-start(), calls=%async_computation.4 | async-start | bytes 4718592 | tf_op jit(solution)/shard_map/reduce_scatter | solution.py:39
  7.2 0.9 copy-start.4
  7.2 2.4 %copy-start.5 = (bf16[128]{0:T(256)(128)(2,1)S(1)}, bf16[128]{0:T(256)(128)(2,1)}, u32[]{:S(2)}) copy-start(bf16[128]{0:T(256)(128)(2,1)} %param.12) | copy-start | bytes 772
  7.2 2.4 %copy-start.6 = (bf16[128]{0:T(256)(128)(2,1)S(1)}, bf16[128]{0:T(256)(128)(2,1)}, u32[]{:S(2)}) copy-start(bf16[128]{0:T(256)(128)(2,1)} %param.10) | copy-start | bytes 772
  10.7 20.9 %all-to-all-start.2 = ((bf16[128,2,2]{1,2,0:T(2,128)(2,1)}), bf16[128,2,2]{1,2,0:T(2,128)(2,1)S(1)}, u32[]{:S(2)}, u32[]{:S(2)}) async-start(bf16[128,2,2]{1,2,0:T(2,128)(2,1)} %copy.29), calls=%async_computation.2 | async-start | bytes 131072 | tf_op jit(solution)/shard_map/all_to_all | solution.py:67
  23.3 13.8 %copy-start.2 = (bf16[128,2048]{1,0:T(8,128)(2,1)S(1)}, bf16[128,2048]{1,0:T(8,128)(2,1)}, u32[]{:S(2)}) copy-start(bf16[128,2048]{1,0:T(8,128)(2,1)} %param.9) | copy-start | bytes 1572868
  23.3 14.0 %copy-start.3 = (bf16[128,2048]{1,0:T(8,128)(2,1)S(1)}, bf16[128,2048]{1,0:T(8,128)(2,1)}, u32[]{:S(2)}) copy-start(bf16[128,2048]{1,0:T(8,128)(2,1)} %param.11) | copy-start | bytes 1572868
  31.7 24.2 %all-to-all-start = ((bf16[128,2,2048]{2,1,0:T(2,128)(2,1)}), bf16[128,2,2048]{2,1,0:T(2,128)(2,1)}, u32[]{:S(2)}, u32[]{:S(2)}) async-start(bf16[128,2,2048]{2,1,0:T(2,128)(2,1)} %convert_element_type.77), calls=%async_computation | async-start | bytes 2097152 | tf_op jit(solution)/shard_map/all_to_all | solution.py:69
  55.9 36.2 %all-to-all-start.1 = ((bf16[128,2,2,2048]{3,2,1,0:T(2,128)(2,1)}), bf16[128,2,2,2048]{3,2,1,0:T(2,128)(2,1)S(1)}, u32[]{:S(2)}, u32[]{:S(2)}) async-start(bf16[128,2,2,2048]{3,2,1,0:T(2,128)(2,1)} %reshape_reshape.6), calls=%async_computation.1 | async-start | bytes 4194304 | tf_op jit(solution)/shard_map/all_to_all | solution.py:66
  61.7 72.0 %all-gather.2.cloned.1.call-start = ((), (), s32[]{:S(2)}) async-start(), calls=%async_computation.5 | async-start | bytes 4718592 | tf_op jit(solution)/shard_map/all_gather | solution.py:86
  104.9 2.2 %copy-start.1 = (bf16[128,2048]{1,0:T(8,128)(2,1)S(1)}, bf16[128,2048]{1,0:T(8,128)(2,1)}, u32[]{:S(2)}) copy-start(bf16[128,2048]{1,0:T(8,128)(2,1)} %reduce-scatter.2.cloned.1.call-done) | copy-start | bytes 1572868
Sparse Core Ops, SparseCore 0:
  10.4 50.0 reduce-scatter.1
  105.0 28.6 all-gather.1
where the time goes:
time: 146 us; the launch traced here: 145 us
  waiting for transfers between devices  74.5 us (51%)
  starting transfers between devices  22.9 us (16%)
  local copies, waits for them, and re-layouts  20.5 us (14%)
  between operations  14.3 us (10%)
  matrix products  7.42 us (5%)
  other arithmetic  5.6 us (4%)
    all_to_all x1, waiting for transfers between devices, local(): lax.all_to_all(code_buffer, ('fsdp', 'dp'), split_axis=0, concat_axis=0,...  27.1 us
    all_gather x1, waiting for transfers between devices, local(): lax.all_gather(master.astype(jnp.bfloat16), 'dp', axis=0, tiled=True)  25.1 us
    all_to_all x1, waiting for transfers between devices, local(): lax.all_to_all(master_buffer.astype(jnp.bfloat16), ('fsdp', 'dp'), split_...  14.7 us
    all_to_all x1, starting transfers between devices, local(): lax.all_to_all(scale_buffer, ('fsdp', 'dp'), split_axis=0, concat_axis=0,...  11.5 us
    unnamed x20, local copies, waits for them, and re-layouts  9.58 us
    all_to_all x1, waiting for transfers between devices, local(): lax.all_to_all(scale_buffer, ('fsdp', 'dp'), split_axis=0, concat_axis=0,...  6.87 us
    all_to_all x1, starting transfers between devices, local(): lax.all_to_all(code_buffer, ('fsdp', 'dp'), split_axis=0, concat_axis=0,...  5.78 us
    all_to_all x1, starting transfers between devices, local(): lax.all_to_all(master_buffer.astype(jnp.bfloat16), ('fsdp', 'dp'), split_...  5.36 us
  transfers between devices with their start and end apart: 5, of which 4 were waited for; matrix products, arithmetic and copies ran while one was open for 17% of the time, Pallas kernels for 0%

commit v1 on v0

--- a/solution.py
+++ b/solution.py
@@ -1,7 +1,39 @@
+import functools
 import jax
 import jax.numpy as jnp
 from jax import lax
 from jax.sharding import PartitionSpec as P
+
+
+def _work_pipes(work_x, pos_dim):
+    kept_arr, piece_now, f_now = (lax.axis_size("dp"), lax.axis_index("dp"), work_x.shape[pos_dim])
+    seen = [it * kept_arr if no == pos_dim else it for no, it in enumerate(work_x.shape)]
+    e_next = lax.dynamic_update_slice_in_dim(
+        jnp.zeros(seen, work_x.dtype), work_x, piece_now * f_now, axis=pos_dim
+    )
+    local_out = local_now = work_x
+    for m in range(1, kept_arr // 2 + 1):
+        local_out = lax.ppermute(
+            local_out,
+            axis_name="dp",
+            perm=list(map(lambda no: (no, (no + 1) % kept_arr), range(kept_arr))),
+        )
+        e_next = lax.dynamic_update_slice_in_dim(
+            e_next, local_out, (piece_now - m) % kept_arr * f_now, axis=pos_dim
+        )
+        if 2 * m < kept_arr:
+            local_now = lax.ppermute(
+                local_now,
+                axis_name="dp",
+                perm=list(map(lambda no: (no, (no - 1) % kept_arr), range(kept_arr))),
+            )
+            e_next = lax.dynamic_update_slice_in_dim(
+                e_next, local_now, (piece_now + m) % kept_arr * f_now, axis=pos_dim
+            )
+    return e_next
+
+
+extend_array = functools.partial(_work_pipes, pos_dim=0)
 
 
 def pair_rank(owners, keyed):
@@ -83,7 +115,7 @@
     square_scales = block_peak(square_next)
     mean_codes = (mean_next / mean_scales.astype(jnp.float32)[:, None]).astype(jnp.bfloat16)
     square_codes = (square_next / square_scales.astype(jnp.float32)[:, None]).astype(jnp.bfloat16)
-    weights = lax.all_gather(master.astype(jnp.bfloat16), "dp", axis=0, tiled=True)
+    weights = extend_array(master.astype(jnp.bfloat16))
     return (weights, master, mean_codes, mean_scales, square_codes, square_scales)
 
 

time: 146 us -> 154 us (1.055)
  the two profiles are of different devices: /device:TPU:1 before, /device:TPU:0 now
where the time goes in v1:
time: 154 us; the launch traced here: 153 us
  waiting for transfers between devices  68.5 us (44%)
  starting transfers between devices  31.7 us (21%)
  local copies, waits for them, and re-layouts  26.1 us (17%)
  between operations  14.3 us (9%)
  other arithmetic  6.57 us (4%)
  matrix products  6.23 us (4%)
    all_to_all x1, waiting for transfers between devices, local(): lax.all_to_all(code_buffer, ('fsdp', 'dp'), split_axis=0, concat_axis=0,...  27.2 us
    ppermute x4, waiting for transfers between devices, _work_pipes(): lax.ppermute(local_out, axis_name='dp', perm=list(map(lambda no: (no, (no...  17.3 us
    all_to_all x1, waiting for transfers between devices, local(): lax.all_to_all(master_buffer.astype(jnp.bfloat16), ('fsdp', 'dp'), split_...  14.6 us
    all_to_all x1, starting transfers between devices, local(): lax.all_to_all(scale_buffer, ('fsdp', 'dp'), split_axis=0, concat_axis=0,...  11.1 us
    ppermute x3, starting transfers between devices, _work_pipes(): lax.ppermute(local_now, axis_name='dp', perm=list(map(lambda no: (no, (no...  8.86 us
    all_to_all x1, waiting for transfers between devices, local(): lax.all_to_all(scale_buffer, ('fsdp', 'dp'), split_axis=0, concat_axis=0,...  6.71 us
    all_to_all x1, starting transfers between devices, local(): lax.all_to_all(code_buffer, ('fsdp', 'dp'), split_axis=0, concat_axis=0,...  5.86 us
    all_to_all x1, starting transfers between devices, local(): lax.all_to_all(master_buffer.astype(jnp.bfloat16), ('fsdp', 'dp'), split_...  5.76 us
  transfers between devices with their start and end apart: 11, of which 8 were waited for; matrix products, arithmetic and copies ran while one was open for 22% of the time, Pallas kernels for 0%

profile of v1, /device:TPU:0, one launch (start us, length us, event | category | flops | bytes accessed | tf_op | source)
XLA Modules:
  0.0 153.3 jit_solution(3978886680655335728)
XLA Ops:
  7.3 0.7 reduce-scatter.2.cloned.1.call-update
  8.1 1.3 select_reduce_fusion
  9.4 0.2 select_reduce_fusion.1
  9.7 0.1 convolution_convert_fusion.3
  9.8 0.2 reshape.115
  10.0 0.7 copy.29
  10.7 11.1 %all-to-all-start.2 = ((bf16[128,2,2]{1,2,0:T(2,128)(2,1)}), bf16[128,2,2]{1,2,0:T(2,128)(2,1)S(1)}, u32[]{:S(2)}, u32[]{:S(2)}) async-start(bf16[128,2,2]{1,2,0:T(2,128)(2,1)} %copy.29), calls=%async_computation.2 | async-start | bytes 131072 | tf_op jit(solution)/shard_map/all_to_all | solution.py:99
  21.8 1.0 convolution_convert_fusion.2
  22.9 1.5 convert_element_type.77
  24.4 6.7 %all-to-all-done.2 = bf16[128,2,2]{1,2,0:T(2,128)(2,1)S(1)} async-done(((bf16[128,2,2]{1,2,0:T(2,128)(2,1)}), bf16[128,2,2]{1,2,0:T(2,128)(2,1)S(1)}, u32[]{:S(2)}, u32[]{:S(2)}) %all-to-all-start.2) | async-done | bytes 1056 | tf_op jit(solution)/shard_map/all_to_all | solution.py:99
  31.1 5.8 %all-to-all-start = ((bf16[128,2,2048]{2,1,0:T(2,128)(2,1)}), bf16[128,2,2048]{2,1,0:T(2,128)(2,1)}, u32[]{:S(2)}, u32[]{:S(2)}) async-start(bf16[128,2,2048]{2,1,0:T(2,128)(2,1)} %convert_element_type.77), calls=%async_computation | async-start | bytes 2097152 | tf_op jit(solution)/shard_map/all_to_all | solution.py:101
  36.9 0.3 copy.26
  37.1 0.3 copy.25
  37.5 0.7 convolution_convert_fusion
  38.2 2.8 %reshape_reshape.6 = bf16[128,2,2,2048]{3,2,1,0:T(2,128)(2,1)} reshape(bf16[256,4096]{1,0:T(8,128)(2,1)S(1)} %convolution_convert_fusion) | data formatting | bytes 4194304 | tf_op jit(solution)/shard_map/reshape;reshape | solution.py:94
  41.0 14.6 %all-to-all-done = bf16[128,2,2048]{2,1,0:T(2,128)(2,1)} async-done(((bf16[128,2,2048]{2,1,0:T(2,128)(2,1)}), bf16[128,2,2048]{2,1,0:T(2,128)(2,1)}, u32[]{:S(2)}, u32[]{:S(2)}) %all-to-all-start) | async-done | bytes 1048608 | tf_op jit(solution)/shard_map/all_to_all | solution.py:101
  55.6 5.9 %all-to-all-start.1 = ((bf16[128,2,2,2048]{3,2,1,0:T(2,128)(2,1)}), bf16[128,2,2,2048]{3,2,1,0:T(2,128)(2,1)S(1)}, u32[]{:S(2)}, u32[]{:S(2)}) async-start(bf16[128,2,2,2048]{3,2,1,0:T(2,128)(2,1)} %reshape_reshape.6), calls=%async_computation.1 | async-start | bytes 4194304 | tf_op jit(solution)/shard_map/all_to_all | solution.py:98
  61.6 0.2 select_reduce_fusion.2
  61.8 0.1 reshape.116
  62.0 0.2 fusion.1
  62.2 2.3 %reshape.113 = bf16[256,2048]{1,0:T(8,128)(2,1)} reshape(bf16[128,2,2048]{2,1,0:T(2,128)(2,1)} %all-to-all-done) | data formatting | bytes 2097152 | tf_op jit(solution)/shard_map/reshape | solution.py:108
  64.5 27.2 %all-to-all-done.1 = bf16[128,2,2,2048]{3,2,1,0:T(2,128)(2,1)S(1)} async-done(((bf16[128,2,2,2048]{3,2,1,0:T(2,128)(2,1)}), bf16[128,2,2,2048]{3,2,1,0:T(2,128)(2,1)S(1)}, u32[]{:S(2)}, u32[]{:S(2)}) %all-to-all-start.1) | async-done | bytes 2097184 | tf_op jit(solution)/shard_map/all_to_all | solution.py:98
  91.7 0.9 copy.34
  92.6 1.8 %fusion = f32[128,4096]{1,0:T(8,128)} fusion(bf16[256,4096]{1,0:T(8,128)(2,1)S(1)} %bitcast.49, s32[128]{0:T(128)S(1)} %multiply_add_fusion.1), kind=kOutput, calls=%fused_computation.3 | convolution fusion | flops 269516800 | bytes 4194816 | tf_op jit(solution)/shard_map/dot_general | solution.py:47
  94.4 1.9 %copy.27 = f32[128,4096]{0,1:T(8,128)S(1)} copy(f32[128,4096]{1,0:T(8,128)} %fusion) | data formatting | bytes 4194304 | tf_op jit(solution)/shard_map/convert_element_type | solution.py:106
  96.3 1.5 fusion.21
  97.8 1.6 %copy.33 = f32[128,1,2048]{2,0,1:T(8,128)S(1)} copy(f32[128,1,2048]{0,2,1:T(8,128)} %get-tuple-element.14) | data formatting | bytes 2097152
  99.4 1.6 %copy.32 = f32[128,1,2048]{2,0,1:T(8,128)S(1)} copy(f32[128,1,2048]{0,2,1:T(8,128)} %get-tuple-element.15) | data formatting | bytes 2097152
  101.0 2.5 %broadcast_in_dim.24 = bf16[1024,2048]{1,0:T(8,128)(2,1)} broadcast(bf16[]{:T(256)} %constant.91.clone.1), dimensions={} | broadcast | bytes 4194306 | tf_op jit(solution)/shard_map/broadcast_in_dim | solution.py:12
  103.5 2.3 %constant_dynamic-update-slice_fusion.6 = (bf16[1024,2048]{1,0:T(8,128)(2,1)}, bf16[128,2048]{1,0:T(8,128)(2,1)}, f32[128,2048]{1,0:T(8,128)}) fusion(bf16[1024,2048]{1,0:T(8,128)(2,1)} %broadcast_in_dim.24, s32[]{:T(128)S(6)} %select_n.109, f32[128]{0:T(128)S(1)} %get-tuple-element.18, f32[128,1,2048]{2,0,1:T(8,128)S(1)} %copy.33, ...), kind=kOutput, calls=%fused_computation.40 | convolution fusion | flops 138706944 | bytes 5768708 | tf_op jit(solution)/shard_map/dot_general | solution.py:52
  105.9 3.0 %collective-permute-start.1 = (bf16[128,2048]{1,0:T(8,128)(2,1)}, bf16[128,2048]{1,0:T(8,128)(2,1)}, u32[]{:S(2)}, u32[]{:S(2)}) collective-permute-start(bf16[128,2048]{1,0:T(8,128)(2,1)} %get-tuple-element.13), channel_id=1, source_target_pairs={{0,7},{1,0},{2,1},{3,2},{4,3},{5,4},{6,5},{7,6},{8,15},{9,8},{10,9... | collective-permute-start | bytes 1572872 | tf_op jit(solution)/shard_map/ppermute | solution.py:25
  108.8 1.6 %fusion.18 = (f32[128]{0:T(128)S(1)}, f32[128]{0:T(128)S(1)}) fusion(bf16[128,2048]{1,0:T(8,128)(2,1)} %reduce-scatter.2.cloned.1.call-done, f32[128]{0:T(128)S(1)} %get-tuple-element.18, f32[128,1,2048]{2,0,1:T(8,128)S(1)} %copy.33, f32[128]{0:T(128)S(1)} %get-tuple-element.19, f32[128,1,2048]{2,0,1:T(8,128)S(1)} %copy.32), kind=kLoop, calls=%fused_computation.62 | loop fusion | flops 3407616 | bytes 2623488 | tf_op jit(solution)/shard_map/reduce_max | solution.py:61
  110.4 0.5 fusion.19
  110.9 5.0 %collective-permute-done = bf16[128,2048]{1,0:T(8,128)(2,1)} collective-permute-done((bf16[128,2048]{1,0:T(8,128)(2,1)}, bf16[128,2048]{1,0:T(8,128)(2,1)}, u32[]{:S(2)}, u32[]{:S(2)}) %collective-permute-start) | collective-permute-done | bytes 524320 | tf_op jit(solution)/shard_map/ppermute | solution.py:16
  116.0 3.0 %collective-permute-start.3 = (bf16[128,2048]{1,0:T(8,128)(2,1)}, bf16[128,2048]{1,0:T(8,128)(2,1)S(1)}, u32[]{:S(2)}, u32[]{:S(2)}) collective-permute-start(bf16[128,2048]{1,0:T(8,128)(2,1)} %collective-permute-done.1), channel_id=1, source_target_pairs={{0,7},{1,0},{2,1},{3,2},{4,3},{5,4},{6,5},{7,6},{8,15},{9,8},{10,9... | collective-permute-start | bytes 1572872 | tf_op jit(solution)/shard_map/ppermute | solution.py:25
  119.0 2.5 %divide_convert_fusion = (bf16[128,2048]{1,0:T(8,128)(2,1)}, bf16[128,2048]{1,0:T(8,128)(2,1)}) fusion(f32[128]{0:T(128)S(1)} %get-tuple-element.8, bf16[128,2048]{1,0:T(8,128)(2,1)} %reduce-scatter.2.cloned.1.call-done, f32[128]{0:T(128)S(1)} %get-tuple-element.18, f32[128,1,2048]{2,0,1:T(8,128)S(1)} %copy.33, f32[128]{0:T(128)S(1)} %get-tuple-element.23, ...), kind=kLoop, calls=%fused_computation.17 | loop fusion | flops 3670016 | bytes 3672064 | tf_op jit(solution)/shard_map/convert_element_type | solution.py:117
  121.4 4.6 %collective-permute-done.2 = bf16[128,2048]{1,0:T(8,128)(2,1)S(1)} collective-permute-done((bf16[128,2048]{1,0:T(8,128)(2,1)}, bf16[128,2048]{1,0:T(8,128)(2,1)S(1)}, u32[]{:S(2)}, u32[]{:S(2)}) %collective-permute-start.2) | collective-permute-done | bytes 524320 | tf_op jit(solution)/shard_map/ppermute | solution.py:16
  126.0 1.9 %constant_dynamic-update-slice_fusion.5 = bf16[1024,2048]{1,0:T(8,128)(2,1)} fusion(bf16[1024,2048]{1,0:T(8,128)(2,1)} %get-tuple-element.12, bf16[128,2048]{1,0:T(8,128)(2,1)} %collective-permute-done, s32[]{:T(128)S(6)} %select_n.111), kind=kLoop, calls=%fused_computation.39 | loop fusion | bytes 1048580 | tf_op jit(solution)/shard_map/dynamic_update_slice | solution.py:21
  127.9 1.9 %constant_dynamic-update-slice_fusion.4 = bf16[1024,2048]{1,0:T(8,128)(2,1)} fusion(bf16[1024,2048]{1,0:T(8,128)(2,1)} %constant_dynamic-update-slice_fusion.5, bf16[128,2048]{1,0:T(8,128)(2,1)} %collective-permute-done.1, s32[]{:T(128)S(6)} %select_n.113), kind=kLoop, calls=%fused_computation.38 | loop fusion | bytes 1048580 | tf_op jit(solution)/shard_map/dynamic_update_slice | solution.py:30
  129.8 3.0 %collective-permute-start.5 = (bf16[128,2048]{1,0:T(8,128)(2,1)S(1)}, bf16[128,2048]{1,0:T(8,128)(2,1)S(1)}, u32[]{:S(2)}, u32[]{:S(2)}) collective-permute-start(bf16[128,2048]{1,0:T(8,128)(2,1)S(1)} %collective-permute-done.3), channel_id=1, source_target_pairs={{0,7},{1,0},{2,1},{3,2},{4,3},{5,4},{6,5},{7,6},{8,15},{9,8},{10,9... | collective-permute-start | bytes 1572872 | tf_op jit(solution)/shard_map/ppermute | solution.py:25
  132.7 0.8 constant_dynamic-update-slice_fusion.3
  133.6 2.3 %collective-permute-done.4 = bf16[128,2048]{1,0:T(8,128)(2,1)S(1)} collective-permute-done((bf16[128,2048]{1,0:T(8,128)(2,1)S(1)}, bf16[128,2048]{1,0:T(8,128)(2,1)S(1)}, u32[]{:S(2)}, u32[]{:S(2)}) %collective-permute-start.4) | collective-permute-done | bytes 524320 | tf_op jit(solution)/shard_map/ppermute | solution.py:16
  135.8 0.8 constant_dynamic-update-slice_fusion.2
  136.7 0.8 constant_dynamic-update-slice_fusion.1
  137.5 1.9 %collective-permute-done.5 = bf16[128,2048]{1,0:T(8,128)(2,1)S(1)} collective-permute-done((bf16[128,2048]{1,0:T(8,128)(2,1)S(1)}, bf16[128,2048]{1,0:T(8,128)(2,1)S(1)}, u32[]{:S(2)}, u32[]{:S(2)}) %collective-permute-start.5) | collective-permute-done | bytes 524320 | tf_op jit(solution)/shard_map/ppermute | solution.py:25
  139.4 0.8 constant_dynamic-update-slice_fusion
  140.3 5.4 %collective-permute-done.6 = bf16[128,2048]{1,0:T(8,128)(2,1)S(1)} collective-permute-done((bf16[128,2048]{1,0:T(8,128)(2,1)S(1)}, bf16[128,2048]{1,0:T(8,128)(2,1)S(1)}, u32[]{:S(2)}, u32[]{:S(2)}) %collective-permute-start.6) | collective-permute-done | bytes 524320 | tf_op jit(solution)/shard_map/ppermute | solution.py:16
  145.7 0.8 constant_dynamic-update-slice_fusion.7
  (32 shorter events, 0.6 us)
Async XLA Ops:
  7.2 14.7 %copy-start = (f32[128,2048]{1,0:T(8,128)S(1)}, f32[128,2048]{1,0:T(8,128)}, u32[]{:S(2)}) copy-start(f32[128,2048]{1,0:T(8,128)} %param.8) | copy-start | bytes 3145732
  7.2 0.9 copy-start.5
  7.2 2.4 %copy-start.6 = (bf16[128]{0:T(256)(128)(2,1)S(1)}, bf16[128]{0:T(256)(128)(2,1)}, u32[]{:S(2)}) copy-start(bf16[128]{0:T(256)(128)(2,1)} %param.12) | copy-start | bytes 772
  7.2 2.4 %copy-start.7 = (bf16[128]{0:T(256)(128)(2,1)S(1)}, bf16[128]{0:T(256)(128)(2,1)}, u32[]{:S(2)}) copy-start(bf16[128]{0:T(256)(128)(2,1)} %param.10) | copy-start | bytes 772
  7.2 93.7 %reduce-scatter.2.cloned.1.call-start = ((), (), s32[]{:S(2)}) async-start(), calls=%async_computation.4 | async-start | bytes 4718592 | tf_op jit(solution)/shard_map/reduce_scatter | solution.py:71
  7.9 28.9 %copy-start.3 = (bf16[128,2048]{1,0:T(8,128)(2,1)S(1)}, bf16[128,2048]{1,0:T(8,128)(2,1)}, u32[]{:S(2)}) copy-start(bf16[128,2048]{1,0:T(8,128)(2,1)} %param.11) | copy-start | bytes 1572868
  8.0 29.2 %copy-start.4 = (bf16[128,2048]{1,0:T(8,128)(2,1)S(1)}, bf16[128,2048]{1,0:T(8,128)(2,1)}, u32[]{:S(2)}) copy-start(bf16[128,2048]{1,0:T(8,128)(2,1)} %param.9) | copy-start | bytes 1572868
  10.7 20.4 %all-to-all-start.2 = ((bf16[128,2,2]{1,2,0:T(2,128)(2,1)}), bf16[128,2,2]{1,2,0:T(2,128)(2,1)S(1)}, u32[]{:S(2)}, u32[]{:S(2)}) async-start(bf16[128,2,2]{1,2,0:T(2,128)(2,1)} %copy.29), calls=%async_computation.2 | async-start | bytes 131072 | tf_op jit(solution)/shard_map/all_to_all | solution.py:99
  31.1 24.5 %all-to-all-start = ((bf16[128,2,2048]{2,1,0:T(2,128)(2,1)}), bf16[128,2,2048]{2,1,0:T(2,128)(2,1)}, u32[]{:S(2)}, u32[]{:S(2)}) async-start(bf16[128,2,2048]{2,1,0:T(2,128)(2,1)} %convert_element_type.77), calls=%async_computation | async-start | bytes 2097152 | tf_op jit(solution)/shard_map/all_to_all | solution.py:101
  55.6 36.1 %all-to-all-start.1 = ((bf16[128,2,2,2048]{3,2,1,0:T(2,128)(2,1)}), bf16[128,2,2,2048]{3,2,1,0:T(2,128)(2,1)S(1)}, u32[]{:S(2)}, u32[]{:S(2)}) async-start(bf16[128,2,2,2048]{3,2,1,0:T(2,128)(2,1)} %reshape_reshape.6), calls=%async_computation.1 | async-start | bytes 4194304 | tf_op jit(solution)/shard_map/all_to_all | solution.py:98
  101.0 2.6 %copy-start.1 = (bf16[128,2048]{1,0:T(8,128)(2,1)S(1)}, bf16[128,2048]{1,0:T(8,128)(2,1)}, u32[]{:S(2)}) copy-start(bf16[128,2048]{1,0:T(8,128)(2,1)} %reduce-scatter.2.cloned.1.call-done) | copy-start | bytes 1572868
  101.0 2.6 %copy-start.2 = (bf16[256,2048]{1,0:T(8,128)(2,1)S(1)}, bf16[256,2048]{1,0:T(8,128)(2,1)}, u32[]{:S(2)}) copy-start(bf16[256,2048]{1,0:T(8,128)(2,1)} %reshape.113) | copy-start | bytes 3145732
  105.9 10.1 %collective-permute-start = (bf16[128,2048]{1,0:T(8,128)(2,1)}, bf16[128,2048]{1,0:T(8,128)(2,1)}, u32[]{:S(2)}, u32[]{:S(2)}) collective-permute-start(bf16[128,2048]{1,0:T(8,128)(2,1)} %get-tuple-element.13), channel_id=1, source_target_pairs={{0,1},{1,2},{2,3},{3,4},{4,5},{5,6},{6,7},{7,0},{8,9},{9,10},{10,1... | collective-permute-start | bytes 1572872 | tf_op jit(solution)/shard_map/ppermute | solution.py:16
  105.9 10.1 %collective-permute-start.1 = (bf16[128,2048]{1,0:T(8,128)(2,1)}, bf16[128,2048]{1,0:T(8,128)(2,1)}, u32[]{:S(2)}, u32[]{:S(2)}) collective-permute-start(bf16[128,2048]{1,0:T(8,128)(2,1)} %get-tuple-element.13), channel_id=1, source_target_pairs={{0,7},{1,0},{2,1},{3,2},{4,3},{5,4},{6,5},{7,6},{8,15},{9,8},{10,9... | collective-permute-start | bytes 1572872 | tf_op jit(solution)/shard_map/ppermute | solution.py:25
  116.0 10.0 %collective-permute-start.2 = (bf16[128,2048]{1,0:T(8,128)(2,1)}, bf16[128,2048]{1,0:T(8,128)(2,1)S(1)}, u32[]{:S(2)}, u32[]{:S(2)}) collective-permute-start(bf16[128,2048]{1,0:T(8,128)(2,1)} %collective-permute-done), channel_id=1, source_target_pairs={{0,1},{1,2},{2,3},{3,4},{4,5},{5,6},{6,7},{7,0},{8,9},{9,10},{10,1... | collective-permute-start | bytes 1572872 | tf_op jit(solution)/shard_map/ppermute | solution.py:16
  116.0 13.8 %collective-permute-start.3 = (bf16[128,2048]{1,0:T(8,128)(2,1)}, bf16[128,2048]{1,0:T(8,128)(2,1)S(1)}, u32[]{:S(2)}, u32[]{:S(2)}) collective-permute-start(bf16[128,2048]{1,0:T(8,128)(2,1)} %collective-permute-done.1), channel_id=1, source_target_pairs={{0,7},{1,0},{2,1},{3,2},{4,3},{5,4},{6,5},{7,6},{8,15},{9,8},{10,9... | collective-permute-start | bytes 1572872 | tf_op jit(solution)/shard_map/ppermute | solution.py:25
  126.0 9.8 %collective-permute-start.4 = (bf16[128,2048]{1,0:T(8,128)(2,1)S(1)}, bf16[128,2048]{1,0:T(8,128)(2,1)S(1)}, u32[]{:S(2)}, u32[]{:S(2)}) collective-permute-start(bf16[128,2048]{1,0:T(8,128)(2,1)S(1)} %collective-permute-done.2), channel_id=1, source_target_pairs={{0,1},{1,2},{2,3},{3,4},{4,5},{5,6},{6,7},{7,0},{8,9},{9,10},{10,1... | collective-permute-start | bytes 1572872 | tf_op jit(solution)/shard_map/ppermute | solution.py:16
  129.8 9.7 %collective-permute-start.5 = (bf16[128,2048]{1,0:T(8,128)(2,1)S(1)}, bf16[128,2048]{1,0:T(8,128)(2,1)S(1)}, u32[]{:S(2)}, u32[]{:S(2)}) collective-permute-start(bf16[128,2048]{1,0:T(8,128)(2,1)S(1)} %collective-permute-done.3), channel_id=1, source_target_pairs={{0,7},{1,0},{2,1},{3,2},{4,3},{5,4},{6,5},{7,6},{8,15},{9,8},{10,9... | collective-permute-start | bytes 1572872 | tf_op jit(solution)/shard_map/ppermute | solution.py:25
  135.8 9.8 %collective-permute-start.6 = (bf16[128,2048]{1,0:T(8,128)(2,1)S(1)}, bf16[128,2048]{1,0:T(8,128)(2,1)S(1)}, u32[]{:S(2)}, u32[]{:S(2)}) collective-permute-start(bf16[128,2048]{1,0:T(8,128)(2,1)S(1)} %collective-permute-done.4), channel_id=1, source_target_pairs={{0,1},{1,2},{2,3},{3,4},{4,5},{5,6},{6,7},{7,0},{8,9},{9,10},{10,1... | collective-permute-start | bytes 1572872 | tf_op jit(solution)/shard_map/ppermute | solution.py:16
Sparse Core Ops, SparseCore 0:
  10.4 50.9 reduce-scatter.1
